TPU v7x, 128 devices: a whole 4x4x4 slice. The times are simulated.
128 devices in a mesh: dp: 16 (over x_lo, z, core), seq: 8 (over x_hi, y).
Axes of the slice: x: 4 (x_hi: 2, x_lo: 2; x = x_hi * 2 + x_lo), y: 4, z: 4, core: 2. Of those that a mesh axis runs over, the one named last changes fastest.
Arguments:
- queries: bfloat16 [16, 2048, 64, 128], P('dp', 'seq')
- keys: bfloat16 [16, 2048, 8, 128], P('dp', 'seq')
- values: bfloat16 [16, 2048, 8, 128], P('dp', 'seq'), may hold values from -6 to 6
- doc_lengths: int32 [16, 16], replicated, may hold values from 1 to 2033, as said below
Outputs:
- attended: bfloat16 [16, 2048, 64, 128], P('dp', 'seq')
Inputs may be any that keep to these rules, and one draw needn't show every extreme that they name: `doc_lengths`: each row sums to 2048; of the sequences s and s + 8, one holds a document of more than 1024 tokens; the least and the most are reached in every draw.
All inputs are finite; a program needn't handle non-finite values.
Results may differ from a plain program's by a relative error of at most 0.003.
Values may be sent and summed in bfloat16 or wider, within the bound.
A program may use at most 192 MiB of HBM per device.

v0:
```python
import functools

import jax
import jax.numpy as jnp
from jax import lax
from jax.experimental import pallas as pl
from jax.experimental.pallas import tpu as pltpu
from jax.sharding import PartitionSpec as P

MESH = pl.DeviceIdType.MESH
LOG2E = 1.4426950408889634
BIG = float(2.0**120)
AHEAD = 2


def attention(docs, lens, q_hbm, k_hbm, v_hbm, o_hbm, qv, raw, wide, kv, ov, q_mark, k_mark,
              send_sem, recv_sem, in_sem, out_sem):
    groups, shards, _, rows, width = kv.shape
    per_group = qv.shape[2]
    half = shards // 2
    dp = lax.axis_index("dp")
    me = lax.axis_index("seq")
    hi = me // half
    y = me % half
    upper = hi == 1
    lower = hi == 0
    right = (y + 1) % half
    left = (y + half - 1) % half

    def q_copy(g):
        return pltpu.make_async_copy(
            q_hbm.at[:, pl.ds(pl.multiple_of(g * per_group, per_group), per_group), :], qv.at[g], in_sem.at[2 + g]
        )

    def o_copy(g):
        return pltpu.make_async_copy(
            ov.at[g], o_hbm.at[:, pl.ds(pl.multiple_of(g * per_group, per_group), per_group), :], out_sem.at[g]
        )

    k_in = pltpu.make_async_copy(k_hbm, raw.at[0], in_sem.at[0])
    v_in = pltpu.make_async_copy(v_hbm, raw.at[1], in_sem.at[1])
    k_in.start()
    v_in.start()
    for g in range(groups):
        q_copy(g).start()

    barrier = pltpu.get_barrier_semaphore()
    for step in range(1, shards):
        pl.semaphore_signal(barrier, inc=1, device_id=(dp, (me + step) % shards), device_id_type=MESH)

    for which, copy in ((0, k_in), (1, v_in)):
        copy.wait()
        wide[...] = raw[which].astype(jnp.float32).reshape(rows * groups, width)
        for g in range(groups):
            kv[g, me, which] = wide[pl.ds(g, rows, stride=groups), :].astype(jnp.bfloat16)

    lane = lax.broadcasted_iota(jnp.int32, (1, width), 1)
    begin = jnp.zeros((1, width), jnp.int32)
    end = jnp.zeros((1, width), jnp.int32)
    so_far = jnp.int32(0)
    for j in range(docs):
        begin = jnp.where(lane == j, so_far, begin)
        so_far = so_far + lens[dp, j]
        end = jnp.where(lane == j, so_far, end)
    for s in range(shards):
        place = s * rows + lax.broadcasted_iota(jnp.int32, (rows, width), 0)
        inside = (place >= begin) & (place < end)
        k_mark[s] = jnp.where(inside, 1.0, 0.0).astype(jnp.bfloat16)
    k_mark[shards] = jnp.where(lax.broadcasted_iota(jnp.int32, (rows, width), 1) == docs, 1.0, 0.0).astype(jnp.bfloat16)
    place = me * rows + lax.broadcasted_iota(jnp.int32, (rows * per_group, width), 0) // per_group
    inside = ((place >= begin) & (place < end)) | (lane > docs)
    q_mark[...] = jnp.where(inside, 0.0, -BIG).astype(jnp.bfloat16)

    pl.semaphore_wait(barrier, shards - 1)

    def remote(g, shard, slot, target):
        return pltpu.make_async_remote_copy(
            src_ref=kv.at[g, shard],
            dst_ref=kv.at[g, shard],
            send_sem=send_sem.at[g, slot],
            recv_sem=recv_sem.at[g, shard],
            device_id=(dp, target),
            device_id_type=MESH,
        )

    own = [
        (lower, me, 0, half + y),
        (lower, me, 1, half + right),
        (lower & (y < 3), me, 2, y + 1),
        (lower & (y < 2), me, 3, y + 2),
        (lower & (y < 1), me, 4, y + 3),
        (upper & (y < 3), me, 0, half + y + 1),
        (upper & (y == 0), me, 1, half + 3),
        (upper & (y == 1), me, 1, half + 3),
    ]
    relayed = [
        (upper, left, 5, half + right),
        (upper, y, 6, half + left),
        (upper & (y == 3), jnp.int32(half), 7, half + 2),
    ]

    def start(table, g):
        for cond, shard, slot, target in table:
            @pl.when(cond)
            def _(shard=shard, slot=slot, target=target):
                remote(g, shard, slot, target).start()

    def arrived(g, shard, cond):
        @pl.when(cond)
        def _():
            remote(g, shard, 0, (me + 1) % shards).wait_recv()

    def relay(g):
        arrived(g, y, upper)
        arrived(g, left, upper)
        arrived(g, jnp.int32(half), upper & (y == 3))
        start(relayed, g)

    def rest(g):
        for s in range(shards - 1):
            early = upper & ((s == y) | (s == left) | ((s == half) & (y == 3)))
            arrived(g, s, (s < me) & jnp.logical_not(early))

    scale = float(width) ** -0.5 * LOG2E
    tile_tokens = 64
    tile = tile_tokens * per_group
    ones = jnp.ones((rows, width), jnp.bfloat16)

    def tile_pass(g, t, pairs):
        q = qv[g, pl.ds(pl.multiple_of(t * tile_tokens, tile_tokens), tile_tokens)].reshape(tile, width)
        marks = q_mark[pl.ds(pl.multiple_of(t * tile, tile), tile), :]
        queries = jnp.concatenate([q, marks], axis=1)
        peak = summed = None
        for p in range(pairs):
            ks, vs = [], []
            for s in (2 * p, 2 * p + 1):
                if s == 0:
                    block = mark = me
                else:
                    block = jnp.where(s <= me, s - 1, me)
                    mark = jnp.where(s <= me, s - 1, shards)
                ks.append(jnp.concatenate([kv[g, block, 0], k_mark[mark]], axis=1))
                vs.append(jnp.concatenate([kv[g, block, 1], ones], axis=1))
            k = jnp.concatenate(ks, axis=0)
            v = jnp.concatenate(vs, axis=0)
            scores = lax.dot_general(queries, k, (((1,), (1,)), ((), ())), preferred_element_type=jnp.float32)
            if p == 0:
                token = t * tile_tokens + lax.broadcasted_iota(jnp.int32, (tile, rows), 0) // per_group
                column = lax.broadcasted_iota(jnp.int32, (tile, rows), 1)
                own_part = jnp.where(column <= token, scores[:, :rows], -BIG)
                scores = jnp.concatenate([own_part, scores[:, rows:]], axis=1)
            top = jnp.max(scores, axis=1, keepdims=True)
            fresh = top if peak is None else jnp.maximum(peak, top)
            weights = jnp.exp2(scores * scale - fresh * scale).astype(jnp.bfloat16)
            product = jnp.dot(weights, v, preferred_element_type=jnp.float32)
            if peak is None:
                summed = product
            else:
                summed = summed * jnp.exp2((peak - fresh) * scale) + product
            peak = fresh
        out = (summed[:, :width] / summed[:, width:]).astype(jnp.bfloat16)
        ov[g, pl.ds(pl.multiple_of(t * tile_tokens, tile_tokens), tile_tokens)] = out.reshape(
            tile_tokens, per_group, width
        )

    def compute(g):
        for pairs in range(1, shards // 2 + 1):
            @pl.when(me // 2 + 1 == pairs)
            def _(pairs=pairs):
                def body(t, _):
                    tile_pass(g, t, pairs)
                    return 0

                lax.fori_loop(0, rows // tile_tokens, body, 0)

    for g in range(AHEAD):
        start(own, g)
    relay(0)

    def head(g, _):
        @pl.when(g + AHEAD < groups)
        def _():
            start(own, g + AHEAD)

        @pl.when(g + 1 < groups)
        def _():
            relay(g + 1)

        rest(g)
        q_copy(g).wait()
        compute(g)
        o_copy(g).start()
        return 0

    lax.fori_loop(0, groups, head, 0)

    def drain(g, _):
        o_copy(g).wait()
        for cond, shard, slot, target in own + relayed:
            @pl.when(cond)
            def _(shard=shard, slot=slot, target=target):
                remote(g, shard, slot, target).wait_send()
        return 0

    lax.fori_loop(0, groups, drain, 0)


def per_device(shards, queries, keys, values, doc_lengths):
    q, k, v = queries[0], keys[0], values[0]
    rows, heads, width = q.shape
    groups = k.shape[1]
    per_group = heads // groups
    docs = doc_lengths.shape[1]
    anywhere = pl.BlockSpec(memory_space=pl.ANY)
    out = pl.pallas_call(
        functools.partial(attention, docs),
        out_shape=jax.ShapeDtypeStruct(q.shape, jnp.bfloat16),
        in_specs=[pl.BlockSpec(memory_space=pltpu.SMEM), anywhere, anywhere, anywhere],
        out_specs=anywhere,
        scratch_shapes=[
            pltpu.VMEM((groups, rows, per_group, width), jnp.bfloat16),
            pltpu.VMEM((2, rows, groups, width), jnp.bfloat16),
            pltpu.VMEM((rows * groups, width), jnp.float32),
            pltpu.VMEM((groups, shards, 2, rows, width), jnp.bfloat16),
            pltpu.VMEM((groups, rows, per_group, width), jnp.bfloat16),
            pltpu.VMEM((rows * per_group, width), jnp.bfloat16),
            pltpu.VMEM((shards + 1, rows, width), jnp.bfloat16),
            pltpu.SemaphoreType.DMA((groups, 8)),
            pltpu.SemaphoreType.DMA((groups, shards)),
            pltpu.SemaphoreType.DMA((2 + groups,)),
            pltpu.SemaphoreType.DMA((groups,)),
        ],
        compiler_params=pltpu.CompilerParams(
            collective_id=0, has_side_effects=True, vmem_limit_bytes=60 * 1024 * 1024
        ),
        name="packed_attention",
    )(doc_lengths, q, k, v)
    return out[None]


def solution(mesh):
    placed = P("dp", "seq", None, None)
    return jax.shard_map(
        functools.partial(per_device, mesh.shape["seq"]),
        mesh=mesh,
        in_specs=(placed, placed, placed, P()),
        out_specs=placed,
        check_vma=False,
    )
```

profile of v0, /device:TPU:126, one launch (start us, length us, event | category | flops | bytes accessed | tf_op | source)
XLA Modules:
  0.0 98.7 jit_solution(11589748795226808955)
XLA Ops:
  0.0 93.6 %packed_attention.1 = bf16[256,64,128]{2,1,0:T(8,128)(2,1)} custom-call(s32[16,16]{1,0:T(8,128)} %lens.1, bf16[256,64,128]{2,1,0:T(8,128)(2,1)} %bitcast.5, bf16[256,8,128]{2,1,0:T(8,128)(2,1)} %bitcast.6, bf16[256,8,128]{2,1,0:T(8,128)(2,1)} %bitcast.7), custom_call_target="tpu_custom_call" | custom-call | tf_op jit(solution)/shard_map/packed_attention/pallas_call | solution.py:215
  93.6 5.2 %copy.6 = bf16[1,256,64,128]{3,2,1,0:T(8,128)(2,1)} copy(bf16[1,256,64,128]{3,2,1,0:T(8,128)(2,1)} %bitcast.4) | data formatting | bytes 8388608
where the time goes:
time: 99.6 us; the launch traced here: 98.7 us
  Pallas kernels  93.6 us (94%)
  local copies, waits for them, and re-layouts  5.16 us (5%)
    pallas_call x1, Pallas kernels, per_device(): pl.pallas_call(functools.partial(attention, docs), out_shape=jax.ShapeDty...  93.6 us
    unnamed x1, local copies, waits for them, and re-layouts  5.16 us

commit v1 on v0

v1 whole, which is shorter than its diff:
```python
import functools

import jax
import jax.numpy as jnp
from jax import lax
from jax.experimental import pallas as pl
from jax.experimental.pallas import tpu as pltpu
from jax.sharding import PartitionSpec as P

MESH = pl.DeviceIdType.MESH
LOG2E = 1.4426950408889634
BIG = float(2.0**120)
AHEAD = 3


def attention(docs, lens, q_hbm, k_hbm, v_hbm, o_hbm, qv, raw, wide, kv, ov, q_mark, k_mark,
              score_a, score_b, weight_a, weight_b, send_sem, recv_sem, in_sem, out_sem):
    groups, shards, _, rows, width = kv.shape
    per_group = qv.shape[2]
    half = shards // 2
    dp = lax.axis_index("dp")
    me = lax.axis_index("seq")
    y = me % half
    upper = me >= half
    lower = me < half
    right = (y + 1) % half
    left = (y + half - 1) % half

    def q_copy(g):
        return pltpu.make_async_copy(
            q_hbm.at[:, pl.ds(pl.multiple_of(g * per_group, per_group), per_group), :], qv.at[g], in_sem.at[2 + g]
        )

    def o_copy(g):
        return pltpu.make_async_copy(
            ov.at[g], o_hbm.at[:, pl.ds(pl.multiple_of(g * per_group, per_group), per_group), :], out_sem.at[g]
        )

    k_in = pltpu.make_async_copy(k_hbm, raw.at[0], in_sem.at[0])
    v_in = pltpu.make_async_copy(v_hbm, raw.at[1], in_sem.at[1])
    k_in.start()
    v_in.start()
    for g in range(groups):
        q_copy(g).start()

    barrier = pltpu.get_barrier_semaphore()
    for step in range(1, shards):
        pl.semaphore_signal(barrier, inc=1, device_id=(dp, (me + step) % shards), device_id_type=MESH)

    for which, copy in ((0, k_in), (1, v_in)):
        copy.wait()
        wide[...] = raw[which].astype(jnp.float32).reshape(rows * groups, width)
        for g in range(groups):
            kv[g, me, which] = wide[pl.ds(g, rows, stride=groups), :].astype(jnp.bfloat16)

    pl.semaphore_wait(barrier, shards - 1)

    def remote(g, shard, slot, target, part=None):
        block = kv.at[g, shard] if part is None else kv.at[g, shard, part]
        return pltpu.make_async_remote_copy(
            src_ref=block,
            dst_ref=block,
            send_sem=send_sem.at[g, slot],
            recv_sem=recv_sem.at[g, shards if part == 1 else shard],
            device_id=(dp, target),
            device_id_type=MESH,
        )

    own = [
        (lower, me, 0, half + y, None),
        (lower, me, 1, right, None),
        (lower & (y < 2), me, 2, y + 2, None),
        (lower & (y < 1), me, 3, y + 3, None),
        (upper & (y < 3), me, 0, half + y + 1, None),
        (upper & (y == 0), me, 1, half + 3, None),
        (upper & (y == 1), me, 1, half + 3, 0),
    ]
    relayed = [
        (lower, left, 4, half + y, None),
        (upper, left, 2, half + right, None),
        (upper, y, 3, half + left, None),
        (upper & (y == 3), jnp.int32(half), 4, half + 2, None),
        (upper & (y == 2), jnp.int32(half + 1), 4, half + 3, 1),
    ]

    def start(table, g):
        for cond, shard, slot, target, part in table:
            @pl.when(cond)
            def _(shard=shard, slot=slot, target=target, part=part):
                remote(g, shard, slot, target, part).start()

    def arrived(g, shard, cond, part=None):
        @pl.when(cond)
        def _():
            remote(g, shard, 0, (me + 1) % shards, part).wait_recv()

    def relay(g):
        arrived(g, left, lower)
        arrived(g, left, upper)
        arrived(g, y, upper)
        arrived(g, jnp.int32(half), upper & (y == 3))
        arrived(g, jnp.int32(half + 1), upper & (y == 2))
        start(relayed, g)

    def rest(g):
        for s in range(shards - 1):
            if s < half:
                arrived(g, s, lower & (s < y - 1))
                arrived(g, s, upper & (s != y) & (s != left))
            elif s == half:
                arrived(g, s, upper & (s < me) & (y != 3))
            elif s == half + 1:
                arrived(g, s, me == shards - 1, 0)
                arrived(g, s, me == shards - 1, 1)
            else:
                arrived(g, s, s < me)

    for g in range(AHEAD):
        start(own, g)

    lane = lax.broadcasted_iota(jnp.int32, (1, width), 1)
    begin = jnp.zeros((1, width), jnp.int32)
    end = jnp.zeros((1, width), jnp.int32)
    so_far = jnp.int32(0)
    for j in range(docs):
        begin = jnp.where(lane == j, so_far, begin)
        so_far = so_far + lens[dp, j]
        end = jnp.where(lane == j, so_far, end)

    def mark_keys(s, _):
        place = s * rows + lax.broadcasted_iota(jnp.int32, (rows, width), 0)
        inside = (place >= begin) & (place < end)
        k_mark[s] = jnp.where(inside, 1.0, 0.0).astype(jnp.bfloat16)
        return 0

    lax.fori_loop(0, shards, mark_keys, 0)

    def mark_queries(s, _):
        spot = s * rows + lax.broadcasted_iota(jnp.int32, (rows, width), 0)
        place = me * rows + spot // per_group
        inside = ((place >= begin) & (place < end)) | (lane >= docs)
        q_mark[pl.ds(pl.multiple_of(s * rows, rows), rows), :] = jnp.where(inside, 0.0, -BIG).astype(jnp.bfloat16)
        return 0

    lax.fori_loop(0, per_group, mark_queries, 0)

    scale = float(width) ** -0.5 * LOG2E
    tile_tokens = 64
    tile = tile_tokens * per_group
    ones = jnp.ones((rows, width), jnp.bfloat16)

    def score_pass(g, t, count, score):
        q = qv[g, pl.ds(pl.multiple_of(t * tile_tokens, tile_tokens), tile_tokens)].reshape(tile, width)
        marks = q_mark[pl.ds(pl.multiple_of(t * tile, tile), tile), :]
        queries = jnp.concatenate([q, marks], axis=1)
        for s in range(count):
            k = jnp.concatenate([kv[g, s, 0], k_mark[s]], axis=1)
            part = lax.dot_general(queries, k, (((1,), (1,)), ((), ())), preferred_element_type=jnp.float32)
            if s == count - 1:
                token = t * tile_tokens + lax.broadcasted_iota(jnp.int32, (tile, rows), 0) // per_group
                column = lax.broadcasted_iota(jnp.int32, (tile, rows), 1)
                part = jnp.where(column <= token, part, -BIG)
            score[:, s * rows : (s + 1) * rows] = part

    def value_pass(g, t, count, score, weight):
        keys = count * rows
        top = jnp.max(score[:, :keys], axis=1, keepdims=True) * scale
        weight[:, :keys] = jnp.exp2(score[:, :keys] * scale - top).astype(jnp.bfloat16)
        v = jnp.concatenate(
            [jnp.concatenate([kv[g, s, 1], ones], axis=1) for s in range(count)], axis=0
        )
        summed = jnp.dot(weight[:, :keys], v, preferred_element_type=jnp.float32)
        out = (summed[:, :width] / summed[:, width:]).astype(jnp.bfloat16)
        ov[g, pl.ds(pl.multiple_of(t * tile_tokens, tile_tokens), tile_tokens)] = out.reshape(
            tile_tokens, per_group, width
        )

    def compute(g, t):
        for count in range(1, shards + 1):
            @pl.when(me == count - 1)
            def _(count=count):
                score_pass(g, t, count, score_a)
                score_pass(g, t + 1, count, score_b)
                value_pass(g, t, count, score_a, weight_a)
                value_pass(g, t + 1, count, score_b, weight_b)

    relay(0)
    relay(1)
    parts = rows // tile_tokens // 2

    def step(n, _):
        g = n // parts
        h = n % parts

        @pl.when(h == 0)
        def _():
            rest(g)
            q_copy(g).wait()

        @pl.when((h == 1) & (g + AHEAD < groups))
        def _():
            start(own, g + AHEAD)

        @pl.when((h == 1) & (g + 2 < groups))
        def _():
            relay(g + 2)

        compute(g, 2 * h)

        @pl.when(h == parts - 1)
        def _():
            o_copy(g).start()

        return 0

    lax.fori_loop(0, groups * parts, step, 0)

    def drain(g, _):
        o_copy(g).wait()
        for cond, shard, slot, target, part in own + relayed:
            @pl.when(cond)
            def _(shard=shard, slot=slot, target=target, part=part):
                remote(g, shard, slot, target, part).wait_send()
        return 0

    lax.fori_loop(0, groups, drain, 0)


def per_device(shards, queries, keys, values, doc_lengths):
    q, k, v = queries[0], keys[0], values[0]
    rows, heads, width = q.shape
    groups = k.shape[1]
    per_group = heads // groups
    docs = doc_lengths.shape[1]
    anywhere = pl.BlockSpec(memory_space=pl.ANY)
    out = pl.pallas_call(
        functools.partial(attention, docs),
        out_shape=jax.ShapeDtypeStruct(q.shape, jnp.bfloat16),
        in_specs=[pl.BlockSpec(memory_space=pltpu.SMEM), anywhere, anywhere, anywhere],
        out_specs=anywhere,
        scratch_shapes=[
            pltpu.VMEM((groups, rows, per_group, width), jnp.bfloat16),
            pltpu.VMEM((2, rows, groups, width), jnp.bfloat16),
            pltpu.VMEM((rows * groups, width), jnp.float32),
            pltpu.VMEM((groups, shards, 2, rows, width), jnp.bfloat16),
            pltpu.VMEM((groups, rows, per_group, width), jnp.bfloat16),
            pltpu.VMEM((rows * per_group, width), jnp.bfloat16),
            pltpu.VMEM((shards, rows, width), jnp.bfloat16),
            pltpu.VMEM((64 * per_group, shards * rows), jnp.float32),
            pltpu.VMEM((64 * per_group, shards * rows), jnp.float32),
            pltpu.VMEM((64 * per_group, shards * rows), jnp.bfloat16),
            pltpu.VMEM((64 * per_group, shards * rows), jnp.bfloat16),
            pltpu.SemaphoreType.DMA((groups, 5)),
            pltpu.SemaphoreType.DMA((groups, shards + 1)),
            pltpu.SemaphoreType.DMA((2 + groups,)),
            pltpu.SemaphoreType.DMA((groups,)),
        ],
        compiler_params=pltpu.CompilerParams(
            collective_id=0, has_side_effects=True, vmem_limit_bytes=60 * 1024 * 1024
        ),
        name="packed_attention",
    )(doc_lengths, q, k, v)
    return out[None]


def solution(mesh):
    placed = P("dp", "seq", None, None)
    return jax.shard_map(
        functools.partial(per_device, mesh.shape["seq"]),
        mesh=mesh,
        in_specs=(placed, placed, placed, P()),
        out_specs=placed,
        check_vma=False,
    )
```

time: 99.6 us -> 85.6 us (0.86)
  Pallas kernels: 93.6 us -> 80.2 us
    pallas_call x1, Pallas kernels: 93.6 us -> 80.2 us  [per_device(): pl.pallas_call(functools.partial(attention, docs), out_shape=jax.ShapeDty...]
where the time goes in v1:
time: 85.6 us; the launch traced here: 85.4 us
  Pallas kernels  80.2 us (94%)
  local copies, waits for them, and re-layouts  5.16 us (6%)
    pallas_call x1, Pallas kernels, per_device(): pl.pallas_call(functools.partial(attention, docs), out_shape=jax.ShapeDty...  80.2 us
    unnamed x1, local copies, waits for them, and re-layouts  5.16 us

profile of v1, /device:TPU:126, one launch (start us, length us, event | category | flops | bytes accessed | tf_op | source)
XLA Modules:
  0.0 85.4 jit_solution(11164357233529824985)
XLA Ops:
  0.0 80.2 %packed_attention.1 = bf16[256,64,128]{2,1,0:T(8,128)(2,1)} custom-call(s32[16,16]{1,0:T(8,128)} %lens.1, bf16[256,64,128]{2,1,0:T(8,128)(2,1)} %bitcast.5, bf16[256,8,128]{2,1,0:T(8,128)(2,1)} %bitcast.6, bf16[256,8,128]{2,1,0:T(8,128)(2,1)} %bitcast.7), custom_call_target="tpu_custom_call" | custom-call | tf_op jit(solution)/shard_map/packed_attention/pallas_call | solution.py:236
  80.2 5.2 %copy.6 = bf16[1,256,64,128]{3,2,1,0:T(8,128)(2,1)} copy(bf16[1,256,64,128]{3,2,1,0:T(8,128)(2,1)} %bitcast.4) | data formatting | bytes 8388608

commit v2 on v1

v2 whole, which is shorter than its diff:
```python
import functools

import jax
import jax.numpy as jnp
from jax import lax
from jax.experimental import pallas as pl
from jax.experimental.pallas import tpu as pltpu
from jax.sharding import PartitionSpec as P

MESH = pl.DeviceIdType.MESH
LOG2E = 1.4426950408889634
BIG = float(2.0**120)
READY = 2
SPREAD_HEAD = 1
TAIL_HEADS = 1


TILE_TOKENS = 64


def head_pass(me, g, t, qv, kv, ov, q_mark, k_mark, scores, weights):
    _, shards, _, rows, width = kv.shape
    per_group = qv.shape[2]
    scale = float(width) ** -0.5 * LOG2E
    tile = TILE_TOKENS * per_group

    def tokens(t):
        return pl.ds(pl.multiple_of(t * TILE_TOKENS, TILE_TOKENS), TILE_TOKENS)

    def score_pass(t, count, score):
        q = qv[g, tokens(t)].reshape(tile, width)
        marks = q_mark[pl.ds(pl.multiple_of(t * tile, tile), tile), :]
        queries = jnp.concatenate([q, marks], axis=1)
        for s in range(count):
            k = jnp.concatenate([kv[g, s, 0], k_mark[s]], axis=1)
            part = lax.dot_general(queries, k, (((1,), (1,)), ((), ())), preferred_element_type=jnp.float32)
            if s == count - 1:
                token = t * TILE_TOKENS + lax.broadcasted_iota(jnp.int32, (tile, rows), 0) // per_group
                column = lax.broadcasted_iota(jnp.int32, (tile, rows), 1)
                part = jnp.where(column <= token, part, -BIG)
            score[:, s * rows : (s + 1) * rows] = part

    def value_pass(t, count, score, weight):
        keys = count * rows
        top = jnp.max(score[:, :keys], axis=1, keepdims=True) * scale
        weight[:, :keys] = jnp.exp2(score[:, :keys] * scale - top).astype(jnp.bfloat16)
        ones = jnp.ones((rows, width), jnp.bfloat16)
        v = jnp.concatenate([jnp.concatenate([kv[g, s, 1], ones], axis=1) for s in range(count)], axis=0)
        summed = jnp.dot(weight[:, :keys], v, preferred_element_type=jnp.float32)
        out = (summed[:, :width] / summed[:, width:]).astype(jnp.bfloat16)
        ov[g, tokens(t)] = out.reshape(TILE_TOKENS, per_group, width)

    for count in range(1, shards + 1):
        @pl.when(me == count - 1)
        def _(count=count):
            for u in range(2):
                score_pass(t + u, count, scores.at[u])
            for u in range(2):
                value_pass(t + u, count, scores.at[u], weights.at[u])


def heads_of(ref, g, per_group, count=1):
    return ref.at[:, pl.ds(g * per_group, count * per_group), :]


def tail(part_hbm, q_hbm, kv_hbm, qm_hbm, km_hbm, o_hbm, qv, kv, ov, done, q_mark, k_mark, scores, weights,
         in_sem, kv_sem, out_sem):
    last, shards, _, rows, width = kv.shape
    per_group = qv.shape[2]
    first = done.shape[1] // per_group
    me = lax.axis_index("seq")
    marks = [pltpu.make_async_copy(km_hbm, k_mark, in_sem.at[0]), pltpu.make_async_copy(qm_hbm, q_mark, in_sem.at[1])]

    def q_copy(g):
        return pltpu.make_async_copy(heads_of(q_hbm, first + g, per_group), qv.at[g], in_sem.at[2 + g])

    def kv_copy(g, s):
        return pltpu.make_async_copy(kv_hbm.at[g, s], kv.at[g, s], kv_sem.at[g, s])

    def o_copy(g):
        return pltpu.make_async_copy(ov.at[g], heads_of(o_hbm, first + g, per_group), out_sem.at[g])

    done_in = pltpu.make_async_copy(heads_of(part_hbm, 0, per_group, first), done, in_sem.at[2 + last])
    done_out = pltpu.make_async_copy(done, heads_of(o_hbm, 0, per_group, first), out_sem.at[last])
    for copy in marks:
        copy.start()
    for g in range(last):
        q_copy(g).start()
        for s in range(shards):
            @pl.when(s <= me)
            def _(g=g, s=s):
                kv_copy(g, s).start()
    done_in.start()
    for copy in marks:
        copy.wait()
    parts = rows // TILE_TOKENS // 2

    def step(n, _):
        g = n // parts
        h = n % parts

        @pl.when(h == 0)
        def _():
            q_copy(g).wait()
            for s in range(shards):
                @pl.when(s <= me)
                def _(s=s):
                    kv_copy(g, s).wait()

        @pl.when(n == 1)
        def _():
            done_in.wait()
            done_out.start()

        head_pass(me, g, 2 * h, qv, kv, ov, q_mark, k_mark, scores, weights)

        @pl.when(h == parts - 1)
        def _():
            o_copy(g).start()

        return 0

    lax.fori_loop(0, last * parts, step, 0)
    for g in range(last):
        o_copy(g).wait()
    done_out.wait()


def attention(docs, lens, q_hbm, k_hbm, v_hbm, o_hbm, kv_hbm, qm_hbm, km_hbm, qv, raw, wide, kv, ov, q_mark, k_mark,
              scores, weights, send_sem, recv_sem, in_sem, out_sem, kv_sem):
    groups, shards, _, rows, width = kv.shape
    here = ov.shape[0]
    per_group = qv.shape[2]
    half = shards // 2
    dp = lax.axis_index("dp")
    me = lax.axis_index("seq")
    y = me % half
    upper = me >= half
    lower = me < half
    right = (y + 1) % half
    left = (y + half - 1) % half

    def q_copy(g):
        return pltpu.make_async_copy(heads_of(q_hbm, g, per_group), qv.at[g], in_sem.at[2 + g])

    def o_copy(g):
        return pltpu.make_async_copy(ov.at[g], heads_of(o_hbm, g, per_group), out_sem.at[g])

    def kv_copy(g, s):
        return pltpu.make_async_copy(kv.at[g, s], kv_hbm.at[g - here, s], kv_sem.at[g - here, s])

    k_in = pltpu.make_async_copy(k_hbm, raw.at[0], in_sem.at[0])
    v_in = pltpu.make_async_copy(v_hbm, raw.at[1], in_sem.at[1])
    k_in.start()
    v_in.start()
    for g in range(here):
        q_copy(g).start()

    barrier = pltpu.get_barrier_semaphore()
    for step in range(1, shards):
        pl.semaphore_signal(barrier, inc=1, device_id=(dp, (me + step) % shards), device_id_type=MESH)

    def own_block(g):
        for which in range(2):
            kv[g, me, which] = wide[which, pl.ds(g, rows, stride=groups), :].astype(jnp.bfloat16)

    for which, copy in ((0, k_in), (1, v_in)):
        copy.wait()
        wide[which] = raw[which].astype(jnp.float32).reshape(rows * groups, width)
    for g in range(READY):
        own_block(g)

    pl.semaphore_wait(barrier, shards - 1)

    def remote(g, shard, slot, target, part=None):
        block = kv.at[g, shard] if part is None else kv.at[g, shard, part]
        return pltpu.make_async_remote_copy(
            src_ref=block,
            dst_ref=block,
            send_sem=send_sem.at[g, slot],
            recv_sem=recv_sem.at[g, shards if part == 1 else shard],
            device_id=(dp, target),
            device_id_type=MESH,
        )

    def spread(g):
        return g == SPREAD_HEAD

    def otherwise(g):
        return jnp.logical_not(spread(g))

    def cross(g):
        return [], [(lower, me, 0, half + y, None)]

    def lower_ring(g):
        return [], [
            (lower, me, 1, right, None),
            (lower & (y < 2), me, 2, y + 2, None),
            (lower & (y < 1), me, 3, y + 3, None),
        ]

    def cross_left(g):
        waits = [(lower, left), (lower & (y == 3) & spread(g), jnp.int32(1))]
        return waits, [
            (lower, left, 4, half + y, None),
            (lower & (y == 3) & spread(g), jnp.int32(1), 3, half + 3, None),
        ]

    def upper_ring_relayed(g):
        return [], [
            (upper & (y == 0), me, 1, half + 3, None),
            (upper & (y == 1), me, 0, half + 2, None),
        ]

    def upper_ring(g):
        return [], [
            (upper & (y == 0), me, 0, half + 1, None),
            (upper & (y == 2), me, 0, half + 3, None),
            (upper & (y == 1) & otherwise(g), me, 1, half + 3, 0),
        ]

    def pass_right(g):
        return [(upper, left)], [(upper & ((y != 2) | otherwise(g)), left, 2, half + right, None)]

    def pass_left(g):
        return [(upper, y)], [(upper, y, 3, half + left, None)]

    def pass_upper(g):
        waits = [(upper & (y == 3), jnp.int32(half)), (upper & (y == 2), jnp.int32(half + 1))]
        return waits, [
            (upper & (y == 3), jnp.int32(half), 4, half + 2, None),
            (upper & (y == 2) & otherwise(g), jnp.int32(half + 1), 4, half + 3, 1),
            (upper & (y == 2) & spread(g), jnp.int32(half + 1), 4, half + 3, None),
        ]

    plan = [
        (upper_ring_relayed, 6), (pass_right, 2), (upper_ring, 8), (pass_upper, 2), (pass_left, 3),
        (cross_left, 4), (lower_ring, 8), (cross, 5),
    ]

    def arrived(g, shard, cond, part=None):
        @pl.when(cond)
        def _():
            remote(g, shard, 0, (me + 1) % shards, part).wait_recv()

    def serve(what, g):
        waits, copies = what(g)
        for cond, shard in waits:
            arrived(g, shard, cond)
        for cond, shard, slot, target, part in copies:
            @pl.when(cond)
            def _(shard=shard, slot=slot, target=target, part=part):
                remote(g, shard, slot, target, part).start()

    def serve_later(g, odd):
        for what, ahead in plan:
            if ahead % 2 == odd:
                later = g + (ahead + odd) // 2

                @pl.when(later < groups)
                def _(what=what, later=later):
                    serve(what, later)

    def rest(g):
        for s in range(shards - 1):
            if s < half:
                early = (y == 3) & spread(g) if s == 1 else False
                arrived(g, s, lower & (s < y - 1) & jnp.logical_not(early))
                arrived(g, s, upper & (s != y) & (s != left))
            elif s == half:
                arrived(g, s, upper & (s < me) & (y != 3))
            elif s == half + 1:
                last = me == shards - 1
                arrived(g, s, last & spread(g))
                arrived(g, s, last & otherwise(g), 0)
                arrived(g, s, last & otherwise(g), 1)
            else:
                arrived(g, s, s < me)

    opening = sorted(
        ((2 * g - ahead, place, what, g) for place, (what, ahead) in enumerate(plan) for g in range(groups) if 2 * g < ahead),
        key=lambda item: item[:2],
    )
    sends = [(what, g) for _, _, what, g in opening if not what(g)[0] and g < READY]
    for what, g in sends:
        serve(what, g)
    for g in range(READY, groups):
        own_block(g)

    lane = lax.broadcasted_iota(jnp.int32, (1, width), 1)
    begin = jnp.zeros((1, width), jnp.int32)
    end = jnp.zeros((1, width), jnp.int32)
    so_far = jnp.int32(0)
    for j in range(docs):
        begin = jnp.where(lane == j, so_far, begin)
        so_far = so_far + lens[dp, j]
        end = jnp.where(lane == j, so_far, end)

    def mark_keys(s, _):
        place = s * rows + lax.broadcasted_iota(jnp.int32, (rows, width), 0)
        inside = (place >= begin) & (place < end)
        k_mark[s] = jnp.where(inside, 1.0, 0.0).astype(jnp.bfloat16)
        return 0

    lax.fori_loop(0, shards, mark_keys, 0)

    def mark_queries(s, _):
        spot = s * rows + lax.broadcasted_iota(jnp.int32, (rows, width), 0)
        place = me * rows + spot // per_group
        inside = ((place >= begin) & (place < end)) | (lane >= docs)
        q_mark[pl.ds(pl.multiple_of(s * rows, rows), rows), :] = jnp.where(inside, 0.0, -BIG).astype(jnp.bfloat16)
        return 0

    lax.fori_loop(0, per_group, mark_queries, 0)
    marks = [pltpu.make_async_copy(k_mark, km_hbm, out_sem.at[here]), pltpu.make_async_copy(q_mark, qm_hbm, out_sem.at[here + 1])]
    for copy in marks:
        copy.start()

    for _, _, what, g in opening:
        if (what, g) not in sends:
            serve(what, g)
    parts = rows // TILE_TOKENS // 2

    def step(n, _):
        g = n // parts
        h = n % parts

        @pl.when(h == 0)
        def _():
            serve_later(g, 0)
            rest(g)

        @pl.when((h == 0) & (g < here))
        def _():
            q_copy(g).wait()

        @pl.when((h == 0) & (g >= here))
        def _():
            for s in range(shards):
                @pl.when(s <= me)
                def _(s=s):
                    kv_copy(g, s).start()

        @pl.when(h == 1)
        def _():
            serve_later(g, 1)

        @pl.when(g < here)
        def _():
            head_pass(me, g, 2 * h, qv, kv, ov, q_mark, k_mark, scores, weights)

        @pl.when((h == parts - 1) & (g < here))
        def _():
            o_copy(g).start()

        return 0

    lax.fori_loop(0, groups * parts, step, 0)
    for copy in marks:
        copy.wait()

    def drain(g, _):
        @pl.when(g < here)
        def _():
            o_copy(g).wait()

        @pl.when(g >= here)
        def _():
            for s in range(shards):
                @pl.when(s <= me)
                def _(s=s):
                    kv_copy(g, s).wait()

        for what, _ in plan:
            for cond, shard, slot, target, part in what(g)[1]:
                @pl.when(cond)
                def _(shard=shard, slot=slot, target=target, part=part):
                    remote(g, shard, slot, target, part).wait_send()
        return 0

    lax.fori_loop(0, groups, drain, 0)


def per_device(shards, queries, keys, values, doc_lengths):
    q, k, v = queries[0], keys[0], values[0]
    rows, heads, width = q.shape
    groups = k.shape[1]
    per_group = heads // groups
    docs = doc_lengths.shape[1]
    here = groups - TAIL_HEADS
    anywhere = pl.BlockSpec(memory_space=pl.ANY)
    tile = TILE_TOKENS * per_group
    bf16 = jnp.bfloat16
    working = [
        pltpu.VMEM((rows * per_group, width), bf16),
        pltpu.VMEM((shards, rows, width), bf16),
        pltpu.VMEM((2, tile, shards * rows), jnp.float32),
        pltpu.VMEM((2, tile, shards * rows), bf16),
    ]
    part, kv_last, q_mark, k_mark = pl.pallas_call(
        functools.partial(attention, docs),
        out_shape=[
            jax.ShapeDtypeStruct(q.shape, bf16),
            jax.ShapeDtypeStruct((TAIL_HEADS, shards, 2, rows, width), bf16),
            jax.ShapeDtypeStruct((rows * per_group, width), bf16),
            jax.ShapeDtypeStruct((shards, rows, width), bf16),
        ],
        in_specs=[pl.BlockSpec(memory_space=pltpu.SMEM), anywhere, anywhere, anywhere],
        out_specs=[anywhere] * 4,
        scratch_shapes=[
            pltpu.VMEM((here, rows, per_group, width), bf16),
            pltpu.VMEM((2, rows, groups, width), bf16),
            pltpu.VMEM((2, rows * groups, width), jnp.float32),
            pltpu.VMEM((groups, shards, 2, rows, width), bf16),
            pltpu.VMEM((here, rows, per_group, width), bf16),
            *working,
            pltpu.SemaphoreType.DMA((groups, 5)),
            pltpu.SemaphoreType.DMA((groups, shards + 1)),
            pltpu.SemaphoreType.DMA((2 + here,)),
            pltpu.SemaphoreType.DMA((here + 2,)),
            pltpu.SemaphoreType.DMA((TAIL_HEADS, shards)),
        ],
        compiler_params=pltpu.CompilerParams(
            collective_id=0, has_side_effects=True, vmem_limit_bytes=60 * 1024 * 1024
        ),
        name="packed_attention",
    )(doc_lengths, q, k, v)
    out = pl.pallas_call(
        tail,
        out_shape=jax.ShapeDtypeStruct(q.shape, bf16),
        in_specs=[anywhere] * 5,
        out_specs=anywhere,
        scratch_shapes=[
            pltpu.VMEM((TAIL_HEADS, rows, per_group, width), bf16),
            pltpu.VMEM((TAIL_HEADS, shards, 2, rows, width), bf16),
            pltpu.VMEM((TAIL_HEADS, rows, per_group, width), bf16),
            pltpu.VMEM((rows, here * per_group, width), bf16),
            *working,
            pltpu.SemaphoreType.DMA((3 + TAIL_HEADS,)),
            pltpu.SemaphoreType.DMA((TAIL_HEADS, shards)),
            pltpu.SemaphoreType.DMA((TAIL_HEADS + 1,)),
        ],
        compiler_params=pltpu.CompilerParams(vmem_limit_bytes=60 * 1024 * 1024),
        name="tail_attention",
    )(part, q, kv_last, q_mark, k_mark)
    return out[None]


def solution(mesh):
    placed = P("dp", "seq", None, None)
    return jax.shard_map(
        functools.partial(per_device, mesh.shape["seq"]),
        mesh=mesh,
        in_specs=(placed, placed, placed, P()),
        out_specs=placed,
        check_vma=False,
    )
```

time: 85.6 us -> 82.4 us (0.963)
  local copies, waits for them, and re-layouts: 5.16 us -> 0 us
  Pallas kernels: 80.2 us -> 82.1 us
    unnamed x1 -> x0, local copies, waits for them, and re-layouts: 5.16 us -> none
    pallas_call x1 -> x2, Pallas kernels: 80.2 us -> 82.1 us  [the longest x1 73.1 us: per_device(): pl.pallas_call(functools.partial(attention, docs), out_shape=[jax.ShapeDt...]
where the time goes in v2:
time: 82.4 us; the launch traced here: 82.3 us
  Pallas kernels  82.1 us (100%)
    pallas_call x1, Pallas kernels, per_device(): pl.pallas_call(functools.partial(attention, docs), out_shape=[jax.ShapeDt...  73.1 us
    pallas_call x1, Pallas kernels, per_device(): pl.pallas_call(tail, out_shape=jax.ShapeDtypeStruct(q.shape, bf16), in_sp...  8.98 us

profile of v2, /device:TPU:126, one launch (start us, length us, event | category | flops | bytes accessed | tf_op | source)
XLA Modules:
  0.0 82.3 jit_solution(14831020667872259572)
XLA Ops:
  0.0 73.1 %packed_attention.1 = (bf16[256,64,128]{2,1,0:T(8,128)(2,1)}, bf16[1,8,2,256,128]{4,3,2,1,0:T(8,128)(2,1)}, bf16[2048,128]{1,0:T(8,128)(2,1)}, bf16[8,256,128]{2,1,0:T(8,128)(2,1)}) custom-call(s32[16,16]{1,0:T(8,128)} %lens.1, bf16[256,64,128]{2,1,0:T(8,128)(2,1)} %bitcast.4, bf16[256,8,128]{2,1,0:T(8,128)(2,1)} %bitcast.6, bf16[256,8,128]{2,1,0:T(8,128)(2,1)} %bitcast.7), custom_call_target="tpu_custom_call" | custom-call | tf_op jit(solution)/shard_map/packed_attention/pallas_call | solution.py:400
  73.1 9.0 %tail_attention.1 = bf16[256,64,128]{2,1,0:T(8,128)(2,1)} custom-call(bf16[256,64,128]{2,1,0:T(8,128)(2,1)} %get-tuple-element.9.part_hbm, bf16[256,64,128]{2,1,0:T(8,128)(2,1)} %bitcast.5, bf16[1,8,2,256,128]{4,3,2,1,0:T(8,128)(2,1)} %get-tuple-element.10.kv_hbm, bf16[2048,128]{1,0:T(8,128)(2,1)} %get-tuple-element.11.qm_hbm, ...), custom_call_target="tpu_custom_call" | custom-call | tf_op jit(solution)/shard_map/tail_attention/pallas_call | solution.py:428

commit v3 on v2

--- a/solution.py
+++ b/solution.py
@@ -77,11 +77,16 @@
     def kv_copy(g, s):
         return pltpu.make_async_copy(kv_hbm.at[g, s], kv.at[g, s], kv_sem.at[g, s])
 
-    def o_copy(g):
-        return pltpu.make_async_copy(ov.at[g], heads_of(o_hbm, first + g, per_group), out_sem.at[g])
+    parts = rows // TILE_TOKENS // 2
+
+    def o_copy(g, h):
+        some = pl.ds(h * (rows // parts), rows // parts)
+        return pltpu.make_async_copy(
+            ov.at[g, some], o_hbm.at[some, pl.ds((first + g) * per_group, per_group), :], out_sem.at[g * parts + h]
+        )
 
     done_in = pltpu.make_async_copy(heads_of(part_hbm, 0, per_group, first), done, in_sem.at[2 + last])
-    done_out = pltpu.make_async_copy(done, heads_of(o_hbm, 0, per_group, first), out_sem.at[last])
+    done_out = pltpu.make_async_copy(done, heads_of(o_hbm, 0, per_group, first), out_sem.at[last * parts])
     for copy in marks:
         copy.start()
     for g in range(last):
@@ -93,7 +98,6 @@
     done_in.start()
     for copy in marks:
         copy.wait()
-    parts = rows // TILE_TOKENS // 2
 
     def step(n, _):
         g = n // parts
@@ -114,15 +118,13 @@
 
         head_pass(me, g, 2 * h, qv, kv, ov, q_mark, k_mark, scores, weights)
 
-        @pl.when(h == parts - 1)
-        def _():
-            o_copy(g).start()
-
+        o_copy(g, h).start()
         return 0
 
     lax.fori_loop(0, last * parts, step, 0)
     for g in range(last):
-        o_copy(g).wait()
+        for h in range(parts):
+            o_copy(g, h).wait()
     done_out.wait()
 
 
@@ -321,6 +323,15 @@
             serve(what, g)
     parts = rows // TILE_TOKENS // 2
 
+    def keep(g, early):
+        for s in range(shards):
+            known = (s == me) | (upper & ((s == y) | (s == left)))
+            wanted = known if early else jnp.logical_not(known)
+
+            @pl.when((g >= here) & (s <= me) & wanted)
+            def _(s=s):
+                kv_copy(g, s).start()
+
     def step(n, _):
         g = n // parts
         h = n % parts
@@ -328,6 +339,7 @@
         @pl.when(h == 0)
         def _():
             serve_later(g, 0)
+            keep(g, True)
             rest(g)
 
         @pl.when((h == 0) & (g < here))
@@ -336,10 +348,7 @@
 
         @pl.when((h == 0) & (g >= here))
         def _():
-            for s in range(shards):
-                @pl.when(s <= me)
-                def _(s=s):
-                    kv_copy(g, s).start()
+            keep(g, False)
 
         @pl.when(h == 1)
         def _():
@@ -438,7 +447,7 @@
             *working,
             pltpu.SemaphoreType.DMA((3 + TAIL_HEADS,)),
             pltpu.SemaphoreType.DMA((TAIL_HEADS, shards)),
-            pltpu.SemaphoreType.DMA((TAIL_HEADS + 1,)),
+            pltpu.SemaphoreType.DMA((TAIL_HEADS * (rows // TILE_TOKENS // 2) + 1,)),
         ],
         compiler_params=pltpu.CompilerParams(vmem_limit_bytes=60 * 1024 * 1024),
         name="tail_attention",

time: 82.4 us -> 82.4 us (level)
  no operation moved by 1% of the time
where the time goes in v3:
time: 82.4 us; the launch traced here: 82.2 us
  Pallas kernels  82.1 us (100%)
    pallas_call x1, Pallas kernels, per_device(): pl.pallas_call(functools.partial(attention, docs), out_shape=[jax.ShapeDt...  73.2 us
    pallas_call x1, Pallas kernels, per_device(): pl.pallas_call(tail, out_shape=jax.ShapeDtypeStruct(q.shape, bf16), in_sp...  8.9 us

profile of v3, /device:TPU:126, one launch (start us, length us, event | category | flops | bytes accessed | tf_op | source)
XLA Modules:
  0.0 82.2 jit_solution(11875276282485717892)
XLA Ops:
  0.0 73.2 %packed_attention.1 = (bf16[256,64,128]{2,1,0:T(8,128)(2,1)}, bf16[1,8,2,256,128]{4,3,2,1,0:T(8,128)(2,1)}, bf16[2048,128]{1,0:T(8,128)(2,1)}, bf16[8,256,128]{2,1,0:T(8,128)(2,1)}) custom-call(s32[16,16]{1,0:T(8,128)} %lens.1, bf16[256,64,128]{2,1,0:T(8,128)(2,1)} %bitcast.4, bf16[256,8,128]{2,1,0:T(8,128)(2,1)} %bitcast.6, bf16[256,8,128]{2,1,0:T(8,128)(2,1)} %bitcast.7), custom_call_target="tpu_custom_call" | custom-call | tf_op jit(solution)/shard_map/packed_attention/pallas_call | solution.py:409
  73.2 8.9 %tail_attention.1 = bf16[256,64,128]{2,1,0:T(8,128)(2,1)} custom-call(bf16[256,64,128]{2,1,0:T(8,128)(2,1)} %get-tuple-element.9.part_hbm, bf16[256,64,128]{2,1,0:T(8,128)(2,1)} %bitcast.5, bf16[1,8,2,256,128]{4,3,2,1,0:T(8,128)(2,1)} %get-tuple-element.10.kv_hbm, bf16[2048,128]{1,0:T(8,128)(2,1)} %get-tuple-element.11.qm_hbm, ...), custom_call_target="tpu_custom_call" | custom-call | tf_op jit(solution)/shard_map/tail_attention/pallas_call | solution.py:437
